TPU v7x, 512 devices: a whole 4x8x8 slice. The times are simulated.
512 devices in a mesh: row: 16 (over y_hi, x), col: 32 (over z, y_lo, core).
Axes of the slice: x: 4, y: 8 (y_hi: 4, y_lo: 2; y = y_hi * 2 + y_lo), z: 8, core: 2. Of those that a mesh axis runs over, the one named last changes fastest.
Arguments:
- query: bfloat16 [16384, 1024], P(('row', 'col')), may hold values from -0.5375 to 0.5375
- passage: bfloat16 [16384, 1024], P(('row', 'col')), may hold values from -0.43 to 0.43
- positive: int32 [512, 32], P(('row', 'col')), may hold values from 0 to 31, each once within a row
Outputs:
- loss_value: float32 [], replicated
- grad_query: bfloat16 [16384, 1024], P(('row', 'col'))
- grad_passage: bfloat16 [16384, 1024], P(('row', 'col'))
Inputs may be any that keep to these rules, and one draw needn't show every extreme that they name: Each row of positive names every position 0 to 31 once.
All inputs are finite; a program needn't handle non-finite values.
Results may differ from a plain program's by a relative error of at most 0.015.
Values may be sent and summed in bfloat16 or wider, within the bound.
No kernel may reach another device: no remote copies, remote signals or barrier semaphores. Data moves between devices by JAX's collectives and lax.ppermute only.
A program may use at most 64 MiB of HBM per device.

v0:
```python
import jax
import jax.numpy as jnp
from jax import lax
from jax.sharding import PartitionSpec as P

logit_scale = 20.0


def tile_scores(query_rows, passage_rows):
    return logit_scale * lax.dot_general(
        query_rows, passage_rows, (((1,), (1,)), ((), ())), preferred_element_type=jnp.float32
    )


def local(query, passage, positive):
    shard_rows = query.shape[0]
    row_devices = lax.axis_size("row")
    col_devices = lax.axis_size("col")
    passage_all = lax.all_gather(passage, "row", axis=0, tiled=True)
    query_all = lax.all_gather(query, "col", axis=0, tiled=True)
    scores = tile_scores(query_all, passage_all)
    row_local_peak = scores.max(axis=1)
    col_local_peak = scores.max(axis=0)
    row_peak = lax.pmax(row_local_peak, "col")
    col_peak = lax.pmax(col_local_peak, "row")
    row_sum = lax.psum(jnp.exp(scores - row_peak[:, None]).sum(axis=1), "col")
    col_sum = lax.psum(jnp.exp(scores - col_peak[None, :]).sum(axis=0), "row")
    row_lse = row_peak + jnp.log(row_sum)
    col_lse = col_peak + jnp.log(col_sum)
    weights = (
        0.5 * (jnp.exp(scores - row_lse[:, None]) + jnp.exp(scores - col_lse[None, :]))
    ).astype(jnp.bfloat16)
    query_sum = lax.psum_scatter(
        jnp.dot(weights, passage_all, preferred_element_type=jnp.float32).astype(jnp.bfloat16),
        "col",
        scatter_dimension=0,
        tiled=True,
    ).astype(jnp.float32)
    passage_sum = lax.psum_scatter(
        lax.dot_general(
            weights, query_all, (((0,), (0,)), ((), ())), preferred_element_type=jnp.float32
        ).astype(jnp.bfloat16),
        "row",
        scatter_dimension=0,
        tiled=True,
    ).astype(jnp.float32)
    slot_index = jnp.arange(shard_rows, dtype=jnp.int32)
    onehot = (positive[0][:, None] == slot_index[None, :]).astype(jnp.bfloat16)
    paired_passage = jnp.dot(onehot, passage, preferred_element_type=jnp.float32)
    paired_query = lax.dot_general(
        onehot, query, (((0,), (0,)), ((), ())), preferred_element_type=jnp.float32
    )
    positive_score = logit_scale * jnp.sum(query.astype(jnp.float32) * paired_passage, axis=1)
    grad_query = (logit_scale * (query_sum - paired_passage)).astype(jnp.bfloat16)
    grad_passage = (logit_scale * (passage_sum - paired_query)).astype(jnp.bfloat16)
    row_part = lax.dynamic_slice_in_dim(row_lse, lax.axis_index("col") * shard_rows, shard_rows)
    col_part = lax.dynamic_slice_in_dim(col_lse, lax.axis_index("row") * shard_rows, shard_rows)
    local_terms = jnp.sum(row_part) + jnp.sum(col_part) - 2.0 * jnp.sum(positive_score)
    summed = lax.psum(local_terms, ("row", "col"))
    loss_value = summed / (2.0 * shard_rows * row_devices * col_devices)
    return (loss_value, grad_query, grad_passage)


def solution(mesh):
    return jax.shard_map(
        local,
        mesh=mesh,
        in_specs=(P(("row", "col"), None), P(("row", "col"), None), P(("row", "col"), None)),
        out_specs=(P(), P(("row", "col"), None), P(("row", "col"), None)),
        check_vma=False,
    )
```

profile of v0, /device:TPU:1, one launch (start us, length us, event | category | flops | bytes accessed | tf_op | source)
XLA Modules:
  0.0 658.9 jit_solution(3152972070807338193)
XLA Ops:
  7.2 0.0 all-gather.5.cloned.1.call-start
  7.2 0.7 all-gather.5.cloned.1.call-update
  7.9 0.0 all-gather.3.cloned.1.call-start
  7.9 0.7 all-gather.3.cloned.1.call-update
  8.6 0.0 reduce-scatter.3.cloned.1.call-start
  8.7 64.2 %all-gather.5.cloned.1.call-done = bf16[512,1024]{1,0:T(8,128)(2,1)} async-done(((bf16[32,1024]{1,0:T(8,128)(2,1)}), bf16[512,1024]{1,0:T(8,128)(2,1)}) %all-gather.5.cloned.1.call-update) | async-done | bytes 1048592 | tf_op jit(solution)/shard_map/all_gather | solution.py:19
  72.9 69.4 %all-gather.3.cloned.1.call-done = bf16[1024,1024]{1,0:T(8,128)(2,1)} async-done(((bf16[32,1024]{1,0:T(8,128)(2,1)}), bf16[1024,1024]{1,0:T(8,128)(2,1)}) %all-gather.3.cloned.1.call-update) | async-done | bytes 2097168 | tf_op jit(solution)/shard_map/all_gather | solution.py:20
  142.3 3.2 fusion.5
  145.5 37.5 %pmax.15 = f32[512]{0:T(512)S(1)} all-reduce(f32[512]{0:T(512)S(1)} %get-tuple-element.5), channel_id=1, replica_groups=mesh['row'=16,'col'=32] {'row'}, use_global_device_ids=true, to_apply=%region_6.0 | all-reduce | flops 512 | bytes 4096 | tf_op jit(solution)/shard_map/pmax | solution.py:25
  183.0 59.6 %pmax.14 = f32[1024]{0:T(1024)S(1)} all-reduce(f32[1024]{0:T(1024)S(1)} %get-tuple-element.6), channel_id=1, replica_groups=mesh['row'=16,'col'=32] {'col'}, use_global_device_ids=true, to_apply=%region_1.0 | all-reduce | flops 1024 | bytes 8192 | tf_op jit(solution)/shard_map/pmax | solution.py:24
  242.6 1.0 exponential_reduce_fusion
  243.5 32.1 %psum.22 = f32[512]{0:T(512)S(1)} all-reduce(f32[512]{0:T(512)S(1)} %get-tuple-element.3), channel_id=1, replica_groups=mesh['row'=16,'col'=32] {'row'}, use_global_device_ids=true, to_apply=%region_8.0 | all-reduce | flops 512 | bytes 4096 | tf_op jit(solution)/shard_map/psum | solution.py:27
  275.7 59.9 %psum.21 = f32[1024]{0:T(1024)S(1)} all-reduce(f32[1024]{0:T(1024)S(1)} %get-tuple-element.4), channel_id=1, replica_groups=mesh['row'=16,'col'=32] {'col'}, use_global_device_ids=true, to_apply=%region_3.0 | all-reduce | flops 1024 | bytes 8192 | tf_op jit(solution)/shard_map/psum | solution.py:26
  335.6 0.0 copy-done.3
  335.6 2.9 convolution_convert_fusion
  338.5 0.0 reduce-scatter.3.cloned.1.call-update
  338.5 0.0 copy-start
  338.5 0.0 copy-start.1
  338.5 0.0 copy-start.2
  338.5 0.0 reduce-scatter.5.cloned.1.call-start
  338.6 4.0 convolution_convert_fusion.1
  342.6 0.0 reduce-scatter.5.cloned.1.call-update
  342.6 0.7 dynamic-slice_reduce_fusion
  343.3 0.7 dynamic-slice_reduce_fusion.1
  345.3 109.5 %reduce-scatter.3.cloned.1.call-done = bf16[32,1024]{1,0:T(8,128)(2,1)} async-done(((bf16[1024,1024]{1,0:T(8,128)(2,1)}), bf16[32,1024]{1,0:T(8,128)(2,1)}) %reduce-scatter.3.cloned.1.call-update) | async-done | bytes 65552 | tf_op jit(solution)/shard_map/reduce_scatter | solution.py:33
  454.8 0.0 copy-done
  454.8 0.0 copy-done.1
  454.8 1.8 multiply_convert_fusion.1
  456.6 0.6 multiply_reduce_fusion.1
  457.8 92.4 %reduce-scatter.5.cloned.1.call-done = bf16[32,1024]{1,0:T(8,128)(2,1)} async-done(((bf16[512,1024]{1,0:T(8,128)(2,1)}), bf16[32,1024]{1,0:T(8,128)(2,1)}) %reduce-scatter.5.cloned.1.call-update) | async-done | bytes 65552 | tf_op jit(solution)/shard_map/reduce_scatter | solution.py:39
  550.2 1.7 fusion.1
  551.9 98.7 %psum.23 = f32[]{:T(128)} all-reduce(f32[]{:T(128)S(6)} %sub.45), channel_id=1, replica_groups=mesh['row'=16,'col'=32] {'row','col'}, use_global_device_ids=true, to_apply=%region_12.0 | all-reduce | flops 1 | bytes 8 | tf_op jit(solution)/shard_map/psum | solution.py:59
  (4 shorter events, 0.0 us)
Async XLA Ops:
  7.2 65.8 %all-gather.5.cloned.1.call-start = ((), (), s32[]{:S(2)}) async-start(), calls=%async_computation.3 | async-start | bytes 1114112 | tf_op jit(solution)/shard_map/all_gather | solution.py:19
  7.9 134.4 %all-gather.3.cloned.1.call-start = ((), (), s32[]{:S(2)}) async-start(), calls=%async_computation.2 | async-start | bytes 2162688 | tf_op jit(solution)/shard_map/all_gather | solution.py:20
  8.6 446.1 %reduce-scatter.3.cloned.1.call-start = ((), (), s32[]{:S(2)}) async-start(), calls=%async_computation.4 | async-start | bytes 2162688 | tf_op jit(solution)/shard_map/reduce_scatter | solution.py:33
  145.5 190.1 %copy-start.3 = (bf16[512,1024]{1,0:T(8,128)(2,1)S(1)}, bf16[512,1024]{1,0:T(8,128)(2,1)}, u32[]{:S(2)}) copy-start(bf16[512,1024]{1,0:T(8,128)(2,1)} %all-gather.5.cloned.1.call-done) | copy-start | bytes 3145732
  338.5 116.3 %copy-start = (bf16[32,1024]{1,0:T(8,128)(2,1)S(1)}, bf16[32,1024]{1,0:T(8,128)(2,1)}, u32[]{:S(2)}) copy-start(bf16[32,1024]{1,0:T(8,128)(2,1)} %param.3) | copy-start | bytes 196612
  338.5 116.3 %copy-start.1 = (bf16[32,1024]{1,0:T(8,128)(2,1)S(1)}, bf16[32,1024]{1,0:T(8,128)(2,1)}, u32[]{:S(2)}) copy-start(bf16[32,1024]{1,0:T(8,128)(2,1)} %param.4) | copy-start | bytes 196612
  338.5 116.2 %copy-start.2 = (s32[1,32]{1,0:T(1,128)S(1)}, s32[1,32]{1,0:T(1,128)}, u32[]{:S(2)}) copy-start(s32[1,32]{1,0:T(1,128)} %param.5) | copy-start | bytes 388
  338.5 211.7 %reduce-scatter.5.cloned.1.call-start = ((), (), s32[]{:S(2)}) async-start(), calls=%async_computation.5 | async-start | bytes 1114112 | tf_op jit(solution)/shard_map/reduce_scatter | solution.py:39
Sparse Core Ops, SparseCore 0:
  11.0 61.9 all-gather.4
  75.1 67.1 all-gather.2
  338.6 116.0 reduce-scatter.2
  458.7 91.4 reduce-scatter.4
where the time goes:
time: 659 us
  waiting for transfers between devices  337 us (51%)
  blocking collectives  288 us (44%)
  between operations  17.5 us (3%)
  matrix products  13.7 us (2%)
    reduce_scatter x1, waiting for transfers between devices, local(): lax.psum_scatter(jnp.dot(weights, passage_all, preferred_element_type=jnp...  109 us
    psum x1, blocking collectives, local(): summed = lax.psum(local_terms, ('row', 'col'))  98.7 us
    reduce_scatter x1, waiting for transfers between devices, local(): lax.psum_scatter(lax.dot_general(weights, query_all, (((0,), (0,)), ((),...  92.4 us
    all_gather x1, waiting for transfers between devices, local(): query_all = lax.all_gather(query, 'col', axis=0, tiled=True)  69.4 us
    all_gather x1, waiting for transfers between devices, local(): passage_all = lax.all_gather(passage, 'row', axis=0, tiled=True)  64.2 us
    psum x1, blocking collectives, local(): row_sum = lax.psum(jnp.exp(scores - row_peak[:, None]).sum(axis=1), 'col')  59.9 us
    pmax x1, blocking collectives, local(): row_peak = lax.pmax(row_local_peak, 'col')  59.6 us
    pmax x1, blocking collectives, local(): col_peak = lax.pmax(col_local_peak, 'row')  37.5 us
  transfers between devices with their start and end apart: 4, of which 4 were waited for; matrix products, arithmetic and copies ran while one was open for 1% of the time, Pallas kernels for 0%

commit v1 on v0

--- a/solution.py
+++ b/solution.py
@@ -16,7 +16,9 @@
     shard_rows = query.shape[0]
     row_devices = lax.axis_size("row")
     col_devices = lax.axis_size("col")
-    passage_all = lax.all_gather(passage, "row", axis=0, tiled=True)
+    passage_all = jnp.concatenate(
+        lax.all_to_all(jnp.stack([passage] * lax.axis_size("row")), "row", 0, 0), axis=0
+    )
     query_all = lax.all_gather(query, "col", axis=0, tiled=True)
     scores = tile_scores(query_all, passage_all)
     row_local_peak = scores.max(axis=1)

time: 659 us -> 602 us (0.914)
  waiting for transfers between devices: 337 us -> 240 us
  blocking collectives: 288 us -> 326 us
    all_gather x1 -> x0, waiting for transfers between devices: 64.2 us -> none  [local(): passage_all = lax.all_gather(passage, 'row', axis=0, tiled=True)]
    all_to_all x0 -> x1, blocking collectives: none -> 40 us  [local(): lax.all_to_all(jnp.stack([passage] * lax.axis_size('row')), 'row', 0, 0)]
    all_gather x1, waiting for transfers between devices: 69.4 us -> 37.9 us  [local(): query_all = lax.all_gather(query, 'col', axis=0, tiled=True)]
  transfers between devices with their start and end apart: 4 -> 3, of which waited for: 4 -> 3; matrix products, arithmetic and copies ran while one was open for 1% -> 1% of each run, Pallas kernels for 0% -> 0%
where the time goes in v1:
time: 602 us; the launch traced here: 601 us
  blocking collectives  326 us (54%)
  waiting for transfers between devices  240 us (40%)
  between operations  17.5 us (3%)
  matrix products  13.5 us (2%)
    reduce_scatter x1, waiting for transfers between devices, local(): lax.psum_scatter(jnp.dot(weights, passage_all, preferred_element_type=jnp...  109 us
    psum x1, blocking collectives, local(): summed = lax.psum(local_terms, ('row', 'col'))  98.7 us
    reduce_scatter x1, waiting for transfers between devices, local(): lax.psum_scatter(lax.dot_general(weights, query_all, (((0,), (0,)), ((),...  92.5 us
    psum x1, blocking collectives, local(): row_sum = lax.psum(jnp.exp(scores - row_peak[:, None]).sum(axis=1), 'col')  59.9 us
    pmax x1, blocking collectives, local(): row_peak = lax.pmax(row_local_peak, 'col')  59.9 us
    all_to_all x1, blocking collectives, local(): lax.all_to_all(jnp.stack([passage] * lax.axis_size('row')), 'row', 0, 0)  40 us
    all_gather x1, waiting for transfers between devices, local(): query_all = lax.all_gather(query, 'col', axis=0, tiled=True)  37.9 us
    pmax x1, blocking collectives, local(): col_peak = lax.pmax(col_local_peak, 'row')  35.8 us
  transfers between devices with their start and end apart: 3, of which 3 were waited for; matrix products, arithmetic and copies ran while one was open for 1% of the time, Pallas kernels for 0%

profile of v1, /device:TPU:1, one launch (start us, length us, event | category | flops | bytes accessed | tf_op | source)
XLA Modules:
  0.0 601.4 jit_solution(7661192494636350631)
XLA Ops:
  7.2 0.0 all-gather.2.cloned.1.call-start
  7.2 0.7 all-gather.2.cloned.1.call-update
  7.9 0.0 reduce-scatter.3.cloned.1.call-start
  7.9 1.0 stack.2
  8.9 40.0 %all_to_all.5 = bf16[16,32,1024]{2,1,0:T(8,128)(2,1)S(1)} all-to-all(bf16[16,32,1024]{2,1,0:T(8,128)(2,1)S(1)} %stack.2), channel_id=1, replica_groups=mesh['row'=16,'col'=32] {'row'}, dimensions={0} | all-to-all | bytes 2097152 | tf_op jit(solution)/shard_map/all_to_all | solution.py:20
  49.0 37.9 %all-gather.2.cloned.1.call-done = bf16[1024,1024]{1,0:T(8,128)(2,1)} async-done(((bf16[32,1024]{1,0:T(8,128)(2,1)}), bf16[1024,1024]{1,0:T(8,128)(2,1)}) %all-gather.2.cloned.1.call-update) | async-done | bytes 2097168 | tf_op jit(solution)/shard_map/all_gather | solution.py:22
  86.9 3.0 fusion.5
  89.8 35.8 %pmax.15 = f32[512]{0:T(512)S(1)} all-reduce(f32[512]{0:T(512)S(1)} %get-tuple-element.5), channel_id=1, replica_groups=mesh['row'=16,'col'=32] {'row'}, use_global_device_ids=true, to_apply=%region_6.0 | all-reduce | flops 512 | bytes 4096 | tf_op jit(solution)/shard_map/pmax | solution.py:27
  125.7 59.9 %pmax.14 = f32[1024]{0:T(1024)S(1)} all-reduce(f32[1024]{0:T(1024)S(1)} %get-tuple-element.6), channel_id=1, replica_groups=mesh['row'=16,'col'=32] {'col'}, use_global_device_ids=true, to_apply=%region_1.0 | all-reduce | flops 1024 | bytes 8192 | tf_op jit(solution)/shard_map/pmax | solution.py:26
  185.5 1.0 exponential_reduce_fusion
  186.5 32.1 %psum.22 = f32[512]{0:T(512)S(1)} all-reduce(f32[512]{0:T(512)S(1)} %get-tuple-element.3), channel_id=1, replica_groups=mesh['row'=16,'col'=32] {'row'}, use_global_device_ids=true, to_apply=%region_8.0 | all-reduce | flops 512 | bytes 4096 | tf_op jit(solution)/shard_map/psum | solution.py:29
  218.6 59.9 %psum.21 = f32[1024]{0:T(1024)S(1)} all-reduce(f32[1024]{0:T(1024)S(1)} %get-tuple-element.4), channel_id=1, replica_groups=mesh['row'=16,'col'=32] {'col'}, use_global_device_ids=true, to_apply=%region_3.0 | all-reduce | flops 1024 | bytes 8192 | tf_op jit(solution)/shard_map/psum | solution.py:28
  278.6 2.9 convolution_convert_fusion
  281.5 0.0 reduce-scatter.3.cloned.1.call-update
  281.5 0.0 copy-start
  281.5 0.0 copy-start.1
  281.5 0.0 copy-start.2
  281.5 0.0 reduce-scatter.5.cloned.1.call-start
  281.6 4.0 convolution_convert_fusion.1
  285.6 0.0 reduce-scatter.5.cloned.1.call-update
  285.7 0.7 dynamic-slice_reduce_fusion
  286.3 0.7 dynamic-slice_reduce_fusion.1
  288.3 108.7 %reduce-scatter.3.cloned.1.call-done = bf16[32,1024]{1,0:T(8,128)(2,1)} async-done(((bf16[1024,1024]{1,0:T(8,128)(2,1)}), bf16[32,1024]{1,0:T(8,128)(2,1)}) %reduce-scatter.3.cloned.1.call-update) | async-done | bytes 65552 | tf_op jit(solution)/shard_map/reduce_scatter | solution.py:35
  397.0 0.0 copy-done
  397.0 0.0 copy-done.1
  397.0 0.0 copy-done.2
  397.0 1.8 multiply_convert_fusion.1
  398.8 0.6 multiply_reduce_fusion.1
  400.1 92.5 %reduce-scatter.5.cloned.1.call-done = bf16[32,1024]{1,0:T(8,128)(2,1)} async-done(((bf16[512,1024]{1,0:T(8,128)(2,1)}), bf16[32,1024]{1,0:T(8,128)(2,1)}) %reduce-scatter.5.cloned.1.call-update) | async-done | bytes 65552 | tf_op jit(solution)/shard_map/reduce_scatter | solution.py:41
  492.6 1.7 fusion.1
  494.4 98.7 %psum.23 = f32[]{:T(128)} all-reduce(f32[]{:T(128)S(6)} %sub.45), channel_id=1, replica_groups=mesh['row'=16,'col'=32] {'row','col'}, use_global_device_ids=true, to_apply=%region_12.0 | all-reduce | flops 1 | bytes 8 | tf_op jit(solution)/shard_map/psum | solution.py:61
  (2 shorter events, 0.0 us)
Async XLA Ops:
  7.2 79.7 %all-gather.2.cloned.1.call-start = ((), (), s32[]{:S(2)}) async-start(), calls=%async_computation.3 | async-start | bytes 2162688 | tf_op jit(solution)/shard_map/all_gather | solution.py:22
  7.9 389.1 %reduce-scatter.3.cloned.1.call-start = ((), (), s32[]{:S(2)}) async-start(), calls=%async_computation.4 | async-start | bytes 2162688 | tf_op jit(solution)/shard_map/reduce_scatter | solution.py:35
  281.5 115.5 %copy-start = (bf16[32,1024]{1,0:T(8,128)(2,1)S(1)}, bf16[32,1024]{1,0:T(8,128)(2,1)}, u32[]{:S(2)}) copy-start(bf16[32,1024]{1,0:T(8,128)(2,1)} %param.3) | copy-start | bytes 196612
  281.5 115.5 %copy-start.1 = (bf16[32,1024]{1,0:T(8,128)(2,1)S(1)}, bf16[32,1024]{1,0:T(8,128)(2,1)}, u32[]{:S(2)}) copy-start(bf16[32,1024]{1,0:T(8,128)(2,1)} %param.4) | copy-start | bytes 196612
  281.5 115.5 %copy-start.2 = (s32[1,32]{1,0:T(1,128)S(1)}, s32[1,32]{1,0:T(1,128)}, u32[]{:S(2)}) copy-start(s32[1,32]{1,0:T(1,128)} %param.5) | copy-start | bytes 388
  281.5 211.1 %reduce-scatter.5.cloned.1.call-start = ((), (), s32[]{:S(2)}) async-start(), calls=%async_computation.5 | async-start | bytes 1114112 | tf_op jit(solution)/shard_map/reduce_scatter | solution.py:41
Sparse Core Ops, SparseCore 0:
  10.1 76.7 all-gather.1
  281.6 115.3 reduce-scatter.2
  401.1 91.4 reduce-scatter.4
